TPU v7x, 32 devices: a whole 2x2x4 slice. The times are simulated.
32 devices in a mesh: px: 8 (over z, y), py: 4 (over x, core).
Axes of the slice: x: 2, y: 2, z: 4, core: 2. Of those that a mesh axis runs over, the one named last changes fastest.
Arguments:
- point_channel_values: bfloat16 [4096, 64, 128], P(('px', 'py')), may hold values from -6 to 6
- point_offsets: bfloat16 [4096, 3, 128], P(('px', 'py')), may hold values from -1 to 17
- point_counts: int32 [4096], P(('px', 'py')), may hold values from 1 to 128
- block_bricks: int32 [4096, 4], P(('px', 'py')), may hold values from 0 to 16383, as said below
- spectral_weights: bfloat16 [2, 32, 32, 32, 64, 128], P(None, None, 'px', 'py'), may hold values from -0.5 to 0.5
- skip_weights: bfloat16 [2, 64, 64], replicated, may hold values from -0.75 to 0.75
- skip_bias: float32 [2, 64], replicated, may hold values from -3 to 3
Outputs:
- decoded: bfloat16 [4096, 64, 128], P(('px', 'py'))
Inputs may be any that keep to these rules, and one draw needn't show every extreme that they name: `block_bricks`: the 4 bricks of a block are distinct and lie on one device. Among the 128 blocks of one device at most 8 have their bricks on any one device, and in every draw some device receives exactly 8 blocks from every device.
All inputs are finite; a program needn't handle non-finite values.
Results may differ from a plain program's by a relative error of at most 0.0075.
Values may be sent and summed in bfloat16 or wider, within the bound.
A program may use at most 256 MiB of HBM per device.

v0:
```python
import math
import jax
import jax.numpy as jnp
from jax import lax
from jax.sharding import PartitionSpec as P

MODES = 32
NX = 128
NY = 128
NZ = 128
LAYERS = 2
AMPLITUDE = 0.25
SPREAD = 4.5
DECODE_SCALE = 0.1
PRECISE = lax.Precision.HIGHEST


def wave_numbers(kept_modes):
    position = jnp.arange(kept_modes, dtype=jnp.int32)
    return jnp.where(position < kept_modes // 2, position, position - kept_modes)


def forward_matrix(length, frequency):
    places = jnp.arange(length, dtype=jnp.int32)
    products = jnp.remainder(places[:, None] * frequency[None, :], length)
    angles = 2.0 * math.pi / length * products.astype(jnp.float32)
    cosine = jnp.cos(angles) / math.sqrt(length)
    sine_part = jnp.sin(angles) / math.sqrt(length)
    from_real = jnp.stack([cosine, -sine_part], axis=-1)
    from_imag = jnp.stack([sine_part, cosine], axis=-1)
    return jnp.stack([from_real, from_imag], axis=1)


def cell_centers():
    cell_index = jnp.arange(128, dtype=jnp.int32)
    return (
        jnp.stack([cell_index // 64, cell_index // 16 % 4, cell_index % 16]).astype(jnp.float32)
        + 0.5
    )


def brick_anchor(local_ids, bricks_y, bricks_z):
    clamped_weights = jnp.maximum(local_ids, 0)
    return jnp.stack(
        [
            2 * (clamped_weights // (bricks_y * bricks_z)),
            4 * (clamped_weights // bricks_z % bricks_y),
            16 * (clamped_weights % bricks_z),
        ],
        axis=-1,
    ).astype(jnp.float32)


def block_work(features, offsets, counts, local_ids, bricks_y, bricks_z):
    total_items, channels, points = features.shape
    group_size = math.gcd(total_items, 16)
    centers = cell_centers()

    def one_group(items):
        feature_share, offset_part, count_part, id_part = items
        validity = (jnp.arange(points, dtype=jnp.int32)[None, :] < count_part[:, None]).astype(
            jnp.float32
        )
        anchors = brick_anchor(id_part, bricks_y, bricks_z)
        relative_position = anchors - anchors[:, :1, :]
        placed = offset_part.astype(jnp.float32)[:, None, :, :] - relative_position[:, :, :, None]
        apart = placed[..., None] - centers[None, None, :, None, :]
        distance = jnp.sum(apart * apart, axis=2)
        kernel_weight_value = (
            AMPLITUDE * jnp.exp(-distance / SPREAD) * validity[:, None, :, None]
        ).astype(jnp.bfloat16)
        brick_tile_grid = jnp.einsum(
            "dqw,dewn->deqn", feature_share, kernel_weight_value, preferred_element_type=jnp.float32
        ).astype(jnp.bfloat16)
        return (kernel_weight_value, brick_tile_grid)

    grouped = tuple(
        (
            member.reshape((total_items // group_size, group_size) + member.shape[1:])
            for member in (features, offsets, counts, local_ids)
        )
    )
    kernel_weight_value, brick_tile_grid = lax.map(one_group, grouped)
    return (
        kernel_weight_value.reshape((total_items,) + kernel_weight_value.shape[2:]),
        brick_tile_grid.reshape((total_items,) + brick_tile_grid.shape[2:]),
    )


def decode_points(brick_values, kernel_weight_value):
    summed = jnp.einsum(
        "nhcx,nhpx->ncp", brick_values, kernel_weight_value, preferred_element_type=jnp.float32
    )
    return (DECODE_SCALE * summed).astype(jnp.bfloat16)


def accumulate(brick_tile_grid, local_ids, bricks_device):
    flat_ids = local_ids.reshape(-1)
    selector = (flat_ids[:, None] == jnp.arange(bricks_device, dtype=jnp.int32)[None, :]).astype(
        jnp.bfloat16
    )
    flat_tiles = brick_tile_grid.reshape((flat_ids.shape[0],) + brick_tile_grid.shape[2:])
    return jnp.einsum("rb,rcx->bcx", selector, flat_tiles, preferred_element_type=jnp.float32)


def to_grid(bricks, bricks_along_first, bricks_y, bricks_z):
    channels = bricks.shape[1]
    shaped = bricks.reshape(bricks_along_first, bricks_y, bricks_z, channels, 2, 4, 16)
    return shaped.transpose(3, 0, 4, 1, 5, 2, 6).reshape(
        channels, 2 * bricks_along_first, 4 * bricks_y, 16 * bricks_z
    )


def to_bricks(grid, bricks_along_first, bricks_y, bricks_z):
    channels = grid.shape[0]
    shaped = grid.reshape(channels, bricks_along_first, 2, bricks_y, 4, bricks_z, 16)
    return shaped.transpose(1, 3, 5, 0, 2, 4, 6).reshape(
        bricks_along_first * bricks_y * bricks_z, channels, 128
    )


def spectral(grid, weights, tables):
    table_third, forward_second, forward_first, back_second, back_first, back_third = tables
    channels, cells_x = (grid.shape[0], grid.shape[1])
    third_modes = jnp.einsum(
        "cxyz,zq->cxyq", grid.astype(jnp.float32), table_third, precision=PRECISE
    ).astype(jnp.bfloat16)
    columns = lax.all_to_all(third_modes, "py", split_axis=3, concat_axis=2, tiled=True)
    third_local = columns.shape[3] // 2
    second_modes = jnp.einsum(
        "cxyzp,ypkq->cxzkq",
        columns.reshape(channels, cells_x, columns.shape[2], third_local, 2).astype(jnp.float32),
        forward_second,
        precision=PRECISE,
    ).astype(jnp.bfloat16)
    row_lines = lax.all_to_all(second_modes, "px", split_axis=3, concat_axis=1, tiled=True)
    first_modes = jnp.einsum(
        "cxzkp,xpmq->mkzcq", row_lines.astype(jnp.float32), forward_first, precision=PRECISE
    ).astype(jnp.bfloat16)
    product = jnp.einsum(
        "mkzcp,mkzcr->mkzpr", first_modes, weights, preferred_element_type=jnp.float32
    )
    product = product.reshape(product.shape[:4] + (2, channels))
    mixed_real = product[:, :, :, 0, 0] - product[:, :, :, 1, 1]
    mixed_imag = product[:, :, :, 0, 1] + product[:, :, :, 1, 0]
    mixed = jnp.stack([mixed_real, mixed_imag], axis=-1)
    first_back = jnp.einsum("mkzcp,mpxq->cxzkq", mixed, back_first, precision=PRECISE).astype(
        jnp.bfloat16
    )
    row_back = lax.all_to_all(first_back, "px", split_axis=1, concat_axis=3, tiled=True)
    second_back = jnp.einsum(
        "cxzkp,kpyq->cxyzq", row_back.astype(jnp.float32), back_second, precision=PRECISE
    )
    second_back = second_back.reshape(channels, cells_x, second_back.shape[2], -1).astype(
        jnp.bfloat16
    )
    column_back = lax.all_to_all(second_back, "py", split_axis=2, concat_axis=3, tiled=True)
    return jnp.einsum(
        "cxyq,qz->cxyz", column_back.astype(jnp.float32), back_third, precision=PRECISE
    )


def slot_plan(block_bricks, bricks_device, slot_total, capacity):
    owners = block_bricks[:, 0] // bricks_device
    order_index = jnp.arange(owners.shape[0], dtype=jnp.int32)
    earlier = (owners[None, :] == owners[:, None]) & (order_index[None, :] < order_index[:, None])
    ranking = jnp.sum(earlier.astype(jnp.int32), axis=1)
    slot_index = owners * capacity + ranking
    matching = slot_index[None, :] == jnp.arange(slot_total, dtype=jnp.int32)[:, None]
    present = jnp.any(matching, axis=1)
    sources = jnp.sum(jnp.where(matching, order_index[None, :], 0), axis=1)
    return (slot_index, present, sources)


def pack_slots(values, present, sources, filler):
    picked = jnp.take(values, sources, axis=0)
    masking = present.reshape((-1,) + (1,) * (values.ndim - 1))
    return jnp.where(masking, picked, jnp.asarray(filler, values.dtype))


def route_back(values):
    return lax.all_to_all(values, ("px", "py"), split_axis=0, concat_axis=0, tiled=True)


def per_device(
    point_channel_values,
    point_offsets,
    point_counts,
    block_bricks,
    spectral_weights,
    skip_weights,
    skip_bias,
):
    mesh_rows = lax.axis_size("px")
    mesh_columns = lax.axis_size("py")
    device_total = mesh_rows * mesh_columns
    capacity = max(2, 2 * point_channel_values.shape[0] // device_total)
    bricks_along_first = NX // mesh_rows // 2
    bricks_y = NY // mesh_columns // 4
    bricks_z = NZ // 16
    bricks_device = bricks_along_first * bricks_y * bricks_z
    slot_total = device_total * capacity
    local_ids = block_bricks % bricks_device
    slot_index, present, sources = slot_plan(block_bricks, bricks_device, slot_total, capacity)
    packed_ids = pack_slots(local_ids, present, sources, -1)
    packed_features = pack_slots(point_channel_values, present, sources, 0)
    packed_offsets = pack_slots(point_offsets, present, sources, 0)
    packed_counts = pack_slots(point_counts, present, sources, 0)
    got_features, got_offsets, got_counts, got_ids = (
        lax.all_to_all(packed_features, ("px", "py"), split_axis=0, concat_axis=0, tiled=True),
        lax.all_to_all(packed_offsets, ("px", "py"), split_axis=0, concat_axis=0, tiled=True),
        lax.all_to_all(packed_counts, ("px", "py"), split_axis=0, concat_axis=0, tiled=True),
        lax.all_to_all(packed_ids, ("px", "py"), split_axis=0, concat_axis=0, tiled=True),
    )
    got_weight, got_tiles = block_work(
        got_features, got_offsets, got_counts, got_ids, bricks_y, bricks_z
    )
    encoded = accumulate(got_tiles, got_ids, bricks_device).astype(jnp.bfloat16)
    grid = to_grid(encoded, bricks_along_first, bricks_y, bricks_z)
    third_matrix = forward_matrix(NZ, jnp.arange(MODES, dtype=jnp.int32))[:, 0]
    weighting = jnp.where(jnp.arange(MODES) == 0, 1.0, 2.0).astype(jnp.float32)
    forward_second = forward_matrix(NY, wave_numbers(MODES))
    forward_first = forward_matrix(NX, wave_numbers(MODES))
    tables = (
        third_matrix.reshape(NZ, 2 * MODES),
        forward_second,
        forward_first,
        forward_second.transpose(2, 3, 0, 1),
        forward_first.transpose(2, 3, 0, 1),
        (third_matrix * weighting[None, :, None]).reshape(NZ, 2 * MODES).T,
    )
    for depth_index in range(LAYERS):
        spectral_part = spectral(grid, spectral_weights[depth_index], tables)
        skipped = jnp.einsum(
            "io,ixyz->oxyz", skip_weights[depth_index], grid, preferred_element_type=jnp.float32
        )
        grid = jax.nn.gelu(
            spectral_part + skipped + skip_bias[depth_index][:, None, None, None], approximate=False
        ).astype(jnp.bfloat16)
    final_bricks = to_bricks(grid, bricks_along_first, bricks_y, bricks_z)
    wanted = jnp.take(final_bricks, jnp.maximum(got_ids, 0), axis=0)
    reply = decode_points(wanted, got_weight)
    returned = route_back(reply)
    return jnp.take(returned, slot_index, axis=0)


def solution(mesh):
    return jax.shard_map(
        per_device,
        mesh=mesh,
        in_specs=(
            P(("px", "py"), None, None),
            P(("px", "py"), None, None),
            P(("px", "py")),
            P(("px", "py"), None),
            P(None, None, "px", "py", None, None),
            P(),
            P(),
        ),
        out_specs=P(("px", "py"), None, None),
        check_vma=False,
    )
```

profile of v0, /device:TPU:0, one launch (start us, length us, event | category | flops | bytes accessed | tf_op | source)
XLA Modules:
  0.0 1413.8 jit_solution(9622906543560222130)
XLA Ops:
  5.5 7.3 all-to-all-start.2
  19.9 4.5 all-to-all-start
  34.5 4.4 select_select_fusion
  38.9 6.2 all-to-all-done.1
  50.8 91.7 %all-to-all-done.3 = bf16[256,64,128]{2,1,0:T(8,128)(2,1)} async-done(((bf16[256,64,128]{2,1,0:T(8,128)(2,1)}), bf16[256,64,128]{2,1,0:T(8,128)(2,1)}, u32[]{:S(2)}, u32[]{:S(2)}) %all-to-all-start.3) | async-done | bytes 4194336 | tf_op jit(solution)/shard_map/all_to_all | solution.py:210
  142.5 154.9 %while.15 = (s32[]{:T(128)}, bf16[16,16,4,128,128]{4,3,2,1,0:T(8,128)(2,1)}, bf16[16,16,4,64,128]{4,3,2,1,0:T(8,128)(2,1)}, bf16[16,16,3,128]{3,2,1,0:T(4,128)(2...) while((s32[]{:T(128)}, ...), condition=%wide.region_5.6_spmd, body=%wide.region_3.5_spmd.sunk | while | flops 151557504 | bytes 16284649 | solution.py:83
  171.8 4.1 multiply_reduce_fusion.2
  297.4 30.3 %fusion.59 = bf16[512,64,128]{2,0,1:T(8,128)(2,1)} fusion(bf16[1024,64,128]{2,1,0:T(8,128)(2,1)} %bitcast.395, s32[1024]{0:T(1024)S(1)} %eq.74), kind=kOutput, calls=%fused_computation.116 | convolution fusion | flops 8594653184 | bytes 25169920 | tf_op jit(solution)/shard_map/rb,rcx->bcx/dot_general | solution.py:103
  327.7 17.6 %copy.421 = bf16[512,64,128]{1,2,0:T(8,128)(2,1)} copy(bf16[512,64,128]{2,0,1:T(8,128)(2,1)} %fusion.59) | data formatting | bytes 16777216 | tf_op jit(solution)/shard_map/convert_element_type | solution.py:218
  345.4 15.1 %copy.422 = bf16[64,8,2,8,4,8,16]{0,6,5,4,3,2,1:T(8,128)(2,1)} copy(bf16[64,8,2,8,4,8,16]{0,6,4,2,5,3,1:T(8,128)(2,1)} %bitcast.354) | data formatting | bytes 16777216 | tf_op jit(solution)/shard_map/transpose | solution.py:109
  360.5 18.9 %copy.424 = bf16[64,16,32,128]{3,2,1,0:T(8,128)(2,1)} copy(bf16[64,16,32,128]{0,3,2,1:T(8,128)(2,1)} %bitcast.350) | data formatting | bytes 16777216 | tf_op jit(solution)/shard_map/reshape | solution.py:109
  379.3 11.1 convolution_convert_fusion.1
  390.4 16.4 %copy.425 = bf16[64,16,32,64]{0,2,1,3:T(8,128)(2,1)} copy(bf16[64,16,32,64]{3,2,1,0:T(8,128)(2,1)} %convolution_convert_fusion.1) | data formatting | bytes 8388608 | tf_op jit(solution)/shard_map/convert_element_type | solution.py:127
  406.8 9.5 reshape.1014
  416.3 5.1 all-to-all-start.4
  421.6 48.0 %all-to-all-done.4 = bf16[4,2,262144]{2,1,0:T(2,128)(2,1)} async-done(((bf16[4,2,262144]{2,1,0:T(2,128)(2,1)}), bf16[4,2,262144]{2,1,0:T(2,128)(2,1)}, u32[]{:S(2)}, u32[]{:S(2)}) %all-to-all-start.4) | async-done | bytes 4194336 | tf_op jit(solution)/shard_map/all_to_all | solution.py:128
  469.6 9.3 reshape.1015
  478.9 9.3 copy.427
  488.1 10.1 copy.484
  498.2 10.3 bitcast_convert_fusion.4
  508.6 7.7 copy.429
  517.9 29.3 %all_to_all.165 = bf16[8,2,32768]{2,1,0:T(2,128)(2,1)} all-to-all(bf16[8,2,32768]{2,1,0:T(2,128)(2,1)S(1)} %reshape.1016), channel_id=1, replica_groups=mesh['px'=8,'py'=4] {'px'}, dimensions={0} | all-to-all | bytes 2097152 | tf_op jit(solution)/shard_map/all_to_all | solution.py:136
  557.1 8.1 fusion.32
  577.3 28.8 %all_to_all.166 = bf16[8,2,32768]{2,1,0:T(2,128)(2,1)S(1)} all-to-all(bf16[8,2,32768]{2,1,0:T(2,128)(2,1)S(1)} %reshape.1018), channel_id=1, replica_groups=mesh['px'=8,'py'=4] {'px'}, dimensions={0} | all-to-all | bytes 2097152 | tf_op jit(solution)/shard_map/all_to_all | solution.py:150
  615.3 4.6 copy.443
  619.9 16.5 %copy.444 = bf16[64,16,128,16]{0,3,1,2:T(8,128)(2,1)} copy(bf16[64,16,128,16]{2,1,3,0:T(8,128)(2,1)} %bitcast.368) | data formatting | bytes 8388608 | tf_op jit(solution)/shard_map/convert_element_type | solution.py:154
  636.4 9.6 reshape.1020
  646.0 5.1 all-to-all-start.7
  651.1 12.8 fusion.106
  663.9 35.3 %all-to-all-done.7 = bf16[4,2,262144]{2,1,0:T(2,128)(2,1)} async-done(((bf16[4,2,262144]{2,1,0:T(2,128)(2,1)}), bf16[4,2,262144]{2,1,0:T(2,128)(2,1)}, u32[]{:S(2)}, u32[]{:S(2)}) %all-to-all-start.7) | async-done | bytes 4194336 | tf_op jit(solution)/shard_map/all_to_all | solution.py:157
  699.2 9.3 reshape.1021
  708.5 9.1 copy.446
  717.6 13.1 copy.448
  730.7 28.6 %fusion.54 = (u16[64,32,128]{2,1,0:T(8,128)(2,1)S(1)}, f32[64,16,32,128]{3,2,1,0:T(8,128)}) fusion(f32[64]{0:T(128)S(1)} %get-tuple-element.225, f32[16,32,128,64]{2,3,1,0:T(8,128)} %fusion.106, bf16[64,16,32,64]{3,2,1,0:T(8,128)(2,1)} %copy.448, f32[128,64,1,1]{0,1,3,2:T(8,128)S(1)} %bitcast.388), kind=kOutput, calls=%fused_computation.104 | convolution fusion | flops 3258712064 | bytes 38306048 | tf_op jit(solution)/shard_map/cxyq,qz->cxyz/dot_general | solution.py:158
  759.3 38.4 %fusion.24 = bf16[64,16,32,128]{3,2,1,0:T(8,128)(2,1)S(1)} fusion(f32[64,16,32,128]{3,2,1,0:T(8,128)} %get-tuple-element.230, u16[64,32,128]{2,1,0:T(8,128)(2,1)S(1)} %get-tuple-element.229), kind=kLoop, calls=%fused_computation.54 | loop fusion | flops 285212672 | bytes 25690112 | tf_op jit(solution)/shard_map/convert_element_type | solution.py:239
  801.0 8.6 convolution_convert_fusion
  809.6 16.4 %copy.452 = bf16[64,16,32,64]{0,2,1,3:T(8,128)(2,1)} copy(bf16[64,16,32,64]{3,2,1,0:T(8,128)(2,1)} %convolution_convert_fusion) | data formatting | bytes 8388608 | tf_op jit(solution)/shard_map/convert_element_type | solution.py:127
  826.0 9.5 reshape.1022
  835.5 54.0 %all_to_all.167 = bf16[4,2,262144]{2,1,0:T(2,128)(2,1)} all-to-all(bf16[4,2,262144]{2,1,0:T(2,128)(2,1)} %reshape.1022), channel_id=1, replica_groups=mesh['px'=8,'py'=4] {'py'}, dimensions={0} | all-to-all | bytes 8388608 | tf_op jit(solution)/shard_map/all_to_all | solution.py:128
  889.5 9.3 reshape.1023
  898.8 9.3 copy.454
  908.0 10.1 copy.496
  918.1 10.4 bitcast_convert_fusion.2
  928.4 7.7 copy.456
  937.8 29.1 %all_to_all.168 = bf16[8,2,32768]{2,1,0:T(2,128)(2,1)} all-to-all(bf16[8,2,32768]{2,1,0:T(2,128)(2,1)S(1)} %reshape.1024), channel_id=1, replica_groups=mesh['px'=8,'py'=4] {'px'}, dimensions={0} | all-to-all | bytes 2097152 | tf_op jit(solution)/shard_map/all_to_all | solution.py:136
  976.8 8.1 fusion.29
  997.2 28.7 %all_to_all.169 = bf16[8,2,32768]{2,1,0:T(2,128)(2,1)S(1)} all-to-all(bf16[8,2,32768]{2,1,0:T(2,128)(2,1)S(1)} %reshape.1026), channel_id=1, replica_groups=mesh['px'=8,'py'=4] {'px'}, dimensions={0} | all-to-all | bytes 2097152 | tf_op jit(solution)/shard_map/all_to_all | solution.py:150
  1035.1 4.6 copy.470
  1039.8 16.5 %copy.471 = bf16[64,16,128,16]{0,3,1,2:T(8,128)(2,1)} copy(bf16[64,16,128,16]{2,1,3,0:T(8,128)(2,1)} %bitcast.369) | data formatting | bytes 8388608 | tf_op jit(solution)/shard_map/convert_element_type | solution.py:154
  1056.3 9.5 reshape.1028
  1065.8 5.0 all-to-all-start.11
  1072.5 15.5 %fusion.56 = f32[16,32,128,64]{2,3,1,0:T(8,128)} fusion(bf16[64,16,32,128]{3,2,1,0:T(8,128)(2,1)} %copy-done.2, bf16[2,64,64]{2,1,0:T(8,128)(2,1)S(1)} %copy-done.7), kind=kOutput, calls=%fused_computation.111 | convolution fusion | flops 536870912 | bytes 25182208 | tf_op jit(solution)/shard_map/io,ixyz->oxyz/dot_general | solution.py:234
  1088.1 30.9 %all-to-all-done.11 = bf16[4,2,262144]{2,1,0:T(2,128)(2,1)} async-done(((bf16[4,2,262144]{2,1,0:T(2,128)(2,1)}), bf16[4,2,262144]{2,1,0:T(2,128)(2,1)}, u32[]{:S(2)}, u32[]{:S(2)}) %all-to-all-start.11) | async-done | bytes 4194336 | tf_op jit(solution)/shard_map/all_to_all | solution.py:157
  1119.0 9.3 reshape.1029
  1128.3 9.1 copy.473
  1137.4 13.1 copy.474
  1150.5 45.9 %fusion.27 = bf16[64,16,32,128]{3,2,1,0:T(8,128)(2,1)} fusion(f32[16,32,128,64]{2,3,1,0:T(8,128)} %fusion.56, bf16[64,16,32,64]{3,2,1,0:T(8,128)(2,1)} %copy.474, f32[128,64,1,1]{0,1,3,2:T(8,128)S(1)} %bitcast.389, f32[64]{0:T(128)S(1)} %get-tuple-element.224), kind=kOutput, calls=%fused_computation.57 | convolution fusion | flops 3502243840 | bytes 29393152 | tf_op jit(solution)/shard_map/cxyq,qz->cxyz/dot_general | solution.py:158
  1196.3 17.7 %copy.478 = bf16[64,16,32,128]{0,3,2,1:T(8,128)(2,1)} copy(bf16[64,16,32,128]{3,2,1,0:T(8,128)(2,1)} %fusion.27) | data formatting | bytes 16777216 | tf_op jit(solution)/shard_map/convert_element_type | solution.py:239
  1214.0 15.3 %copy.479 = bf16[8,8,8,64,2,4,16]{3,6,5,4,2,1,0:T(8,128)(2,1)} copy(bf16[8,8,8,64,2,4,16]{3,6,2,5,1,4,0:T(8,128)(2,1)} %bitcast.355) | data formatting | bytes 16777216 | tf_op jit(solution)/shard_map/transpose | solution.py:117
  1229.3 26.6 %gather_fusion.4 = bf16[1024,64,128]{1,2,0:T(8,128)(2,1)} fusion(bf16[512,64,128]{1,2,0:T(8,128)(2,1)} %bitcast.353, s32[1024]{0:T(1024)S(1)} %copy-done.3), kind=kCustom, calls=%fused_computation.4 | custom fusion | bytes 33558528 | tf_op jit(solution)/shard_map/jit(_take)/gather | solution.py:241
  1255.9 30.5 %copy.481 = bf16[256,4,64,128]{3,2,1,0:T(8,128)(2,1)} copy(bf16[256,4,64,128]{2,3,1,0:T(8,128)(2,1)} %bitcast.352) | data formatting | bytes 33554432 | tf_op jit(solution)/shard_map/jit(_take)/gather | solution.py:241
  1286.4 22.2 %fusion.55 = bf16[256,64,128]{2,1,0:T(8,128)(2,1)} fusion(bf16[256,4,128,128]{3,2,1,0:T(8,128)(2,1)} %bitcast.394, bf16[256,4,64,128]{3,2,1,0:T(8,128)(2,1)} %copy.481, pred[256,4]{1,0:T(8,128)(4,1)S(1)} %bitcast.390), kind=kOutput, calls=%fused_computation.106 | convolution fusion | flops 2160066560 | bytes 54526976 | tf_op jit(solution)/shard_map/nhcx,nhpx->ncp/dot_general | solution.py:91
  1312.9 93.2 %all-to-all-done.12 = bf16[256,64,128]{2,1,0:T(8,128)(2,1)} async-done(((bf16[256,64,128]{2,1,0:T(8,128)(2,1)}), bf16[256,64,128]{2,1,0:T(8,128)(2,1)}, u32[]{:S(2)}, u32[]{:S(2)}) %all-to-all-start.12) | async-done | bytes 4194336 | tf_op jit(solution)/shard_map/all_to_all | solution.py:182
  1406.1 4.3 gather_fusion.5
  (339 shorter events, 256.3 us)
Async XLA Ops:
  0.0 24.6 %copy-start = (bf16[128,64,128]{2,1,0:T(8,128)(2,1)S(1)}, bf16[128,64,128]{2,1,0:T(8,128)(2,1)}, u32[]{:S(2)}) copy-start(bf16[128,64,128]{2,1,0:T(8,128)(2,1)} %param.9) | copy-start | bytes 6291460
  1.7 0.8 copy-start.9
  5.5 14.4 %all-to-all-start.2 = ((s32[32,8,1]{1,2,0:T(1,128)}), s32[32,8,1]{1,2,0:T(1,128)S(1)}, u32[]{:S(2)}, u32[]{:S(2)}) async-start(s32[32,8,1]{1,2,0:T(1,128)} %bitcast.34), calls=%async_computation.2 | async-start | bytes 32768 | tf_op jit(solution)/shard_map/all_to_all | solution.py:212
  19.9 12.0 all-to-all-start
  31.9 110.6 %copy-start.4 = (s32[32,8,4]{1,2,0:T(4,128)}, s32[32,8,4]{1,2,0:T(4,128)S(1)}, u32[]{:S(2)}) copy-start(s32[32,8,4]{1,2,0:T(4,128)S(1)} %all-to-all-done) | copy-start | bytes 12292
  31.9 13.2 all-to-all-start.1
  45.0 97.5 %all-to-all-start.3 = ((bf16[256,64,128]{2,1,0:T(8,128)(2,1)}), bf16[256,64,128]{2,1,0:T(8,128)(2,1)}, u32[]{:S(2)}, u32[]{:S(2)}) async-start(bf16[256,64,128]{2,1,0:T(8,128)(2,1)} %select_select_fusion), calls=%async_computation.3 | async-start | bytes 8388608 | tf_op jit(solution)/shard_map/all_to_all | solution.py:210
  416.3 53.3 %all-to-all-start.4 = ((bf16[4,2,262144]{2,1,0:T(2,128)(2,1)}), bf16[4,2,262144]{2,1,0:T(2,128)(2,1)}, u32[]{:S(2)}, u32[]{:S(2)}) async-start(bf16[4,2,262144]{2,1,0:T(2,128)(2,1)} %reshape.1014), calls=%async_computation.4 | async-start | bytes 8388608 | tf_op jit(solution)/shard_map/all_to_all | solution.py:128
  619.9 31.2 %copy-start.8 = (f32[2,64]{1,0:T(2,128)S(1)}, f32[2,64]{1,0:T(2,128)}, u32[]{:S(2)}) copy-start(f32[2,64]{1,0:T(2,128)} %param.15) | copy-start | bytes 1540
  619.9 31.2 %copy-start.7 = (bf16[2,64,64]{2,1,0:T(8,128)(2,1)S(1)}, bf16[2,64,64]{2,1,0:T(8,128)(2,1)}, u32[]{:S(2)}) copy-start(bf16[2,64,64]{2,1,0:T(8,128)(2,1)} %param.14) | copy-start | bytes 49156
  646.0 53.2 %all-to-all-start.7 = ((bf16[4,2,262144]{2,1,0:T(2,128)(2,1)}), bf16[4,2,262144]{2,1,0:T(2,128)(2,1)}, u32[]{:S(2)}, u32[]{:S(2)}) async-start(bf16[4,2,262144]{2,1,0:T(2,128)(2,1)} %reshape.1020), calls=%async_computation.7 | async-start | bytes 8388608 | tf_op jit(solution)/shard_map/all_to_all | solution.py:157
  797.7 3.2 copy-start.2
  1039.8 31.0 %copy-start.5 = (s32[32,8,4]{1,2,0:T(4,128)S(1)}, s32[32,8,4]{1,2,0:T(4,128)}, u32[]{:S(2)}) copy-start(s32[32,8,4]{1,2,0:T(4,128)} %copy-done.4) | copy-start | bytes 12292
  1065.8 53.2 %all-to-all-start.11 = ((bf16[4,2,262144]{2,1,0:T(2,128)(2,1)}), bf16[4,2,262144]{2,1,0:T(2,128)(2,1)}, u32[]{:S(2)}, u32[]{:S(2)}) async-start(bf16[4,2,262144]{2,1,0:T(2,128)(2,1)} %reshape.1028), calls=%async_computation.11 | async-start | bytes 8388608 | tf_op jit(solution)/shard_map/all_to_all | solution.py:157
  1214.0 15.3 %copy-start.3 = (s32[1024]{0:T(1024)S(1)}, s32[1024]{0:T(1024)}, u32[]{:S(2)}) copy-start(s32[1024]{0:T(1024)} %broadcast_clamp_fusion) | copy-start | bytes 12292
  1255.9 30.5 %copy-start.6 = (pred[32,8,4]{2,1,0:T(8,128)(4,1)S(1)}, pred[32,8,4]{2,1,0:T(8,128)(4,1)}, u32[]{:S(2)}) copy-start(pred[32,8,4]{2,1,0:T(8,128)(4,1)} %copy.505) | copy-start | bytes 3076
  1286.4 25.8 %copy-start.10 = (s32[128]{0:T(128)S(1)}, s32[128]{0:T(128)}, u32[]{:S(2)}) copy-start(s32[128]{0:T(128)} %copy-done.9) | copy-start | bytes 1540
  1286.4 127.2 %copy-start.1 = (bf16[128,64,128]{2,1,0:T(8,128)(2,1)S(1)}, bf16[128,64,128]{2,1,0:T(8,128)(2,1)}, u32[]{:S(2)}) copy-start(bf16[128,64,128]{2,1,0:T(8,128)(2,1)} %param.9) | copy-start | bytes 6291460
  1308.6 97.5 %all-to-all-start.12 = ((bf16[256,64,128]{2,1,0:T(8,128)(2,1)}), bf16[256,64,128]{2,1,0:T(8,128)(2,1)}, u32[]{:S(2)}, u32[]{:S(2)}) async-start(bf16[256,64,128]{2,1,0:T(8,128)(2,1)} %fusion.55), calls=%async_computation.12 | async-start | bytes 8388608 | tf_op jit(solution)/shard_map/all_to_all | solution.py:182
where the time goes:
time: 1430 us; the launch traced here: 1410 us
  local copies, waits for them, and re-layouts  462 us (32%)
  waiting for transfers between devices  310 us (22%)
  matrix products  273 us (19%)
  blocking collectives  170 us (12%)
  other arithmetic  160 us (11%)
  starting transfers between devices  36.7 us (3%)
    unnamed x39, local copies, waits for them, and re-layouts  97.6 us
    all_to_all x1, waiting for transfers between devices, route_back(): lax.all_to_all(values, ('px', 'py'), split_axis=0, concat_axis=0, tiled=T...  93.2 us
    all_to_all x1, waiting for transfers between devices, per_device(): lax.all_to_all(packed_features, ('px', 'py'), split_axis=0, concat_axis=0...  91.7 us
    dot_general x2, matrix products, spectral(): jnp.einsum('cxyq,qz->cxyz', column_back.astype(jnp.float32), back_third,...  74.5 us
    all_to_all x2, waiting for transfers between devices, spectral(): lax.all_to_all(second_back, 'py', split_axis=2, concat_axis=3, tiled=True)  66.3 us
    reduce_sum x16, other arithmetic, one_group(): distance = jnp.sum(apart * apart, axis=2)  65.9 us
    all_to_all x2, blocking collectives, spectral(): lax.all_to_all(second_modes, 'px', split_axis=3, concat_axis=1, tiled=True)  58.4 us
    all_to_all x2, blocking collectives, spectral(): lax.all_to_all(first_back, 'px', split_axis=1, concat_axis=3, tiled=True)  57.6 us
  transfers between devices with their start and end apart: 8, of which 8 were waited for; matrix products, arithmetic and copies ran while one was open for 3% of the time, Pallas kernels for 0%

commit v1 on v0

--- a/solution.py
+++ b/solution.py
@@ -13,6 +13,15 @@
 SPREAD = 4.5
 DECODE_SCALE = 0.1
 PRECISE = lax.Precision.HIGHEST
+apply_forms = lambda slab_in: jnp.concatenate(
+    lax.all_to_all(
+        jnp.stack(jnp.split(slab_in, lax.axis_size("py"), axis=3), axis=0),
+        "py",
+        split_axis=0,
+        concat_axis=0,
+    ),
+    axis=2,
+)
 
 
 def wave_numbers(kept_modes):
@@ -125,7 +134,7 @@
     third_modes = jnp.einsum(
         "cxyz,zq->cxyq", grid.astype(jnp.float32), table_third, precision=PRECISE
     ).astype(jnp.bfloat16)
-    columns = lax.all_to_all(third_modes, "py", split_axis=3, concat_axis=2, tiled=True)
+    columns = apply_forms(third_modes)
     third_local = columns.shape[3] // 2
     second_modes = jnp.einsum(
         "cxyzp,ypkq->cxzkq",

time: 1430 us -> 1530 us (1.070)
  local copies, waits for them, and re-layouts: 462 us -> 558 us
    another operation x0 -> x12, local copies, waits for them, and re-layouts: none -> 133 us  [the longest x10 113 us: jnp.stack(jnp.split(slab_in, lax.axis_size('py'), axis=3), axis=0)]
    convert_element_type x2 -> x0, local copies, waits for them, and re-layouts: 32.7 us -> none  [spectral(): third_modes = jnp.einsum('cxyz,zq->cxyq', grid.astype(jnp.float32), table...]
    all_to_all x2 -> x0, local copies, waits for them, and re-layouts: 18.5 us -> none  [spectral(): lax.all_to_all(third_modes, 'py', split_axis=3, concat_axis=2, tiled=True)]
    reshape x2 -> x4, local copies, waits for them, and re-layouts: 20.1 us -> 36.7 us  [jnp.concatenate(lax.all_to_all(jnp.stack(jnp.split(slab_in, lax.axis_size...]
    unnamed x39 -> x43, local copies, waits for them, and re-layouts: 97.6 us -> 94.2 us
where the time goes in v1:
time: 1530 us; the launch traced here: 1520 us
  local copies, waits for them, and re-layouts  558 us (36%)
  waiting for transfers between devices  309 us (20%)
  matrix products  270 us (18%)
  other arithmetic  175 us (11%)
  blocking collectives  170 us (11%)
  starting transfers between devices  36.9 us (2%)
    another operation x10, local copies, waits for them, and re-layouts, jnp.stack(jnp.split(slab_in, lax.axis_size('py'), axis=3), axis=0)  113 us
    unnamed x43, local copies, waits for them, and re-layouts  94.2 us
    all_to_all x1, waiting for transfers between devices, route_back(): lax.all_to_all(values, ('px', 'py'), split_axis=0, concat_axis=0, tiled=T...  93.2 us
    all_to_all x1, waiting for transfers between devices, per_device(): lax.all_to_all(packed_features, ('px', 'py'), split_axis=0, concat_axis=0...  91.2 us
    dot_general x2, matrix products, spectral(): jnp.einsum('cxyq,qz->cxyz', column_back.astype(jnp.float32), back_third,...  74.5 us
    reduce_sum x16, other arithmetic, one_group(): distance = jnp.sum(apart * apart, axis=2)  65.9 us
    all_to_all x2, waiting for transfers between devices, spectral(): lax.all_to_all(second_back, 'py', split_axis=2, concat_axis=3, tiled=True)  65.7 us
    all_to_all x2, blocking collectives, spectral(): lax.all_to_all(second_modes, 'px', split_axis=3, concat_axis=1, tiled=True)  58.1 us
  transfers between devices with their start and end apart: 8, of which 8 were waited for; matrix products, arithmetic and copies ran while one was open for 3% of the time, Pallas kernels for 0%

profile of v1, /device:TPU:0, one launch (start us, length us, event | category | flops | bytes accessed | tf_op | source)
XLA Modules:
  0.0 1520.2 jit_solution(2514492749766168289)
XLA Ops:
  5.5 7.3 all-to-all-start.2
  51.3 91.2 %all-to-all-done.3 = bf16[256,64,128]{2,1,0:T(8,128)(2,1)} async-done(((bf16[256,64,128]{2,1,0:T(8,128)(2,1)}), bf16[256,64,128]{2,1,0:T(8,128)(2,1)}, u32[]{:S(2)}, u32[]{:S(2)}) %all-to-all-start.3) | async-done | bytes 4194336 | tf_op jit(solution)/shard_map/all_to_all | solution.py:219
  142.5 155.0 %while.15 = (s32[]{:T(128)}, bf16[16,16,4,128,128]{4,3,2,1,0:T(8,128)(2,1)}, bf16[16,16,4,64,128]{4,3,2,1,0:T(8,128)(2,1)}, bf16[16,16,3,128]{3,2,1,0:T(4,128)(2...) while((s32[]{:T(128)}, ...), condition=%wide.region_5.6_spmd, body=%wide.region_3.5_spmd.sunk | while | flops 151557504 | bytes 16284649 | solution.py:92
  297.5 30.0 %fusion.59 = bf16[512,64,128]{2,0,1:T(8,128)(2,1)} fusion(bf16[1024,64,128]{2,1,0:T(8,128)(2,1)} %bitcast.409, s32[1024]{0:T(1024)S(1)} %eq.74), kind=kOutput, calls=%fused_computation.126 | convolution fusion | flops 8594653184 | bytes 25169920 | tf_op jit(solution)/shard_map/rb,rcx->bcx/dot_general | solution.py:112
  327.5 17.6 %copy.435 = bf16[512,64,128]{1,2,0:T(8,128)(2,1)} copy(bf16[512,64,128]{2,0,1:T(8,128)(2,1)} %fusion.59) | data formatting | bytes 16777216 | tf_op jit(solution)/shard_map/convert_element_type | solution.py:227
  345.1 15.1 copy.436
  360.2 19.0 %copy.438 = bf16[64,16,32,128]{3,2,1,0:T(8,128)(2,1)} copy(bf16[64,16,32,128]{0,3,2,1:T(8,128)(2,1)} %bitcast.368) | data formatting | bytes 16777216 | tf_op jit(solution)/shard_map/reshape | solution.py:118
  379.2 9.1 convolution_convert_fusion.1
  388.3 13.1 slice_bitcast_fusion.7
  401.4 10.1 copy.439
  411.5 11.1 copy.440
  422.6 11.1 copy.441
  433.7 11.1 copy.442
  452.0 9.5 reshape.1012
  466.9 48.0 %all-to-all-done.4 = bf16[4,2,262144]{2,1,0:T(2,128)(2,1)} async-done(((bf16[4,2,262144]{2,1,0:T(2,128)(2,1)}), bf16[4,2,262144]{2,1,0:T(2,128)(2,1)}, u32[]{:S(2)}, u32[]{:S(2)}) %all-to-all-start.4) | async-done | bytes 4194336 | tf_op jit(solution)/shard_map/all_to_all | solution.py:17
  514.9 9.3 reshape.1013
  524.2 9.2 bitcast_bitcast_fusion.1
  533.4 9.1 copy.443
  542.5 10.1 copy.502
  552.6 10.4 bitcast_convert_fusion.4
  563.0 7.7 copy.445
  572.4 29.0 %all_to_all.145 = bf16[8,2,32768]{2,1,0:T(2,128)(2,1)} all-to-all(bf16[8,2,32768]{2,1,0:T(2,128)(2,1)S(1)} %reshape.1014), channel_id=1, replica_groups=mesh['px'=8,'py'=4] {'px'}, dimensions={0} | all-to-all | bytes 2097152 | tf_op jit(solution)/shard_map/all_to_all | solution.py:145
  611.3 8.1 fusion.32
  631.7 28.9 %all_to_all.146 = bf16[8,2,32768]{2,1,0:T(2,128)(2,1)S(1)} all-to-all(bf16[8,2,32768]{2,1,0:T(2,128)(2,1)S(1)} %reshape.1016), channel_id=1, replica_groups=mesh['px'=8,'py'=4] {'px'}, dimensions={0} | all-to-all | bytes 2097152 | tf_op jit(solution)/shard_map/all_to_all | solution.py:159
  674.4 16.5 %copy.460 = bf16[64,16,128,16]{0,3,1,2:T(8,128)(2,1)} copy(bf16[64,16,128,16]{2,1,3,0:T(8,128)(2,1)} %bitcast.382) | data formatting | bytes 8388608 | tf_op jit(solution)/shard_map/convert_element_type | solution.py:163
  691.0 9.6 reshape.1018
  706.2 12.8 fusion.106
  719.0 34.8 %all-to-all-done.7 = bf16[4,2,262144]{2,1,0:T(2,128)(2,1)} async-done(((bf16[4,2,262144]{2,1,0:T(2,128)(2,1)}), bf16[4,2,262144]{2,1,0:T(2,128)(2,1)}, u32[]{:S(2)}, u32[]{:S(2)}) %all-to-all-start.7) | async-done | bytes 4194336 | tf_op jit(solution)/shard_map/all_to_all | solution.py:166
  753.8 9.3 reshape.1019
  763.1 9.1 copy.462
  772.2 13.1 copy.464
  785.3 28.6 %fusion.54 = (u16[64,32,128]{2,1,0:T(8,128)(2,1)S(1)}, f32[64,16,32,128]{3,2,1,0:T(8,128)}) fusion(f32[64]{0:T(128)S(1)} %get-tuple-element.233, f32[16,32,128,64]{2,3,1,0:T(8,128)} %fusion.106, bf16[64,16,32,64]{3,2,1,0:T(8,128)(2,1)} %copy.464, f32[128,64,1,1]{0,1,3,2:T(8,128)S(1)} %bitcast.402), kind=kOutput, calls=%fused_computation.104 | convolution fusion | flops 3258712064 | bytes 38306048 | tf_op jit(solution)/shard_map/cxyq,qz->cxyz/dot_general | solution.py:167
  813.9 38.4 %fusion.24 = bf16[64,16,32,128]{3,2,1,0:T(8,128)(2,1)S(1)} fusion(f32[64,16,32,128]{3,2,1,0:T(8,128)} %get-tuple-element.238, u16[64,32,128]{2,1,0:T(8,128)(2,1)S(1)} %get-tuple-element.237), kind=kLoop, calls=%fused_computation.54 | loop fusion | flops 285212672 | bytes 25690112 | tf_op jit(solution)/shard_map/convert_element_type | solution.py:248
  859.5 13.2 slice_bitcast_fusion.3
  872.7 10.1 copy.468
  882.8 11.1 copy.469
  893.9 11.1 copy.470
  905.0 11.1 copy.471
  916.0 7.2 fusion.128
  923.3 9.5 reshape.1020
  932.8 54.0 %all_to_all.147 = bf16[4,2,262144]{2,1,0:T(2,128)(2,1)} all-to-all(bf16[4,2,262144]{2,1,0:T(2,128)(2,1)} %reshape.1020), channel_id=1, replica_groups=mesh['px'=8,'py'=4] {'py'}, dimensions={0} | all-to-all | bytes 8388608 | tf_op jit(solution)/shard_map/all_to_all | solution.py:17
  986.8 9.3 reshape.1021
  996.0 9.2 bitcast_bitcast_fusion
  1005.3 9.1 copy.472
  1014.4 10.0 copy.514
  1024.5 10.4 bitcast_convert_fusion.2
  1034.8 7.7 copy.474
  1044.2 29.1 %all_to_all.148 = bf16[8,2,32768]{2,1,0:T(2,128)(2,1)} all-to-all(bf16[8,2,32768]{2,1,0:T(2,128)(2,1)S(1)} %reshape.1022), channel_id=1, replica_groups=mesh['px'=8,'py'=4] {'px'}, dimensions={0} | all-to-all | bytes 2097152 | tf_op jit(solution)/shard_map/all_to_all | solution.py:145
  1083.2 8.1 fusion.29
  1103.6 28.7 %all_to_all.149 = bf16[8,2,32768]{2,1,0:T(2,128)(2,1)S(1)} all-to-all(bf16[8,2,32768]{2,1,0:T(2,128)(2,1)S(1)} %reshape.1024), channel_id=1, replica_groups=mesh['px'=8,'py'=4] {'px'}, dimensions={0} | all-to-all | bytes 2097152 | tf_op jit(solution)/shard_map/all_to_all | solution.py:159
  1146.1 16.5 %copy.489 = bf16[64,16,128,16]{0,3,1,2:T(8,128)(2,1)} copy(bf16[64,16,128,16]{2,1,3,0:T(8,128)(2,1)} %bitcast.383) | data formatting | bytes 8388608 | tf_op jit(solution)/shard_map/convert_element_type | solution.py:163
  1162.6 9.5 reshape.1026
  1178.9 15.5 %fusion.56 = f32[16,32,128,64]{2,3,1,0:T(8,128)} fusion(bf16[64,16,32,128]{3,2,1,0:T(8,128)(2,1)} %copy-done.2, bf16[2,64,64]{2,1,0:T(8,128)(2,1)S(1)} %copy-done.8), kind=kOutput, calls=%fused_computation.121 | convolution fusion | flops 536870912 | bytes 25182208 | tf_op jit(solution)/shard_map/io,ixyz->oxyz/dot_general | solution.py:243
  1194.4 30.9 %all-to-all-done.11 = bf16[4,2,262144]{2,1,0:T(2,128)(2,1)} async-done(((bf16[4,2,262144]{2,1,0:T(2,128)(2,1)}), bf16[4,2,262144]{2,1,0:T(2,128)(2,1)}, u32[]{:S(2)}, u32[]{:S(2)}) %all-to-all-start.11) | async-done | bytes 4194336 | tf_op jit(solution)/shard_map/all_to_all | solution.py:166
  1225.3 9.3 reshape.1027
  1234.7 9.1 copy.491
  1243.8 13.1 copy.492
  1256.9 45.9 %fusion.27 = bf16[64,16,32,128]{3,2,1,0:T(8,128)(2,1)} fusion(f32[16,32,128,64]{2,3,1,0:T(8,128)} %fusion.56, bf16[64,16,32,64]{3,2,1,0:T(8,128)(2,1)} %copy.492, f32[128,64,1,1]{0,1,3,2:T(8,128)S(1)} %bitcast.403, f32[64]{0:T(128)S(1)} %copy-done.12), kind=kOutput, calls=%fused_computation.57 | convolution fusion | flops 3502243840 | bytes 29393152 | tf_op jit(solution)/shard_map/cxyq,qz->cxyz/dot_general | solution.py:167
  1302.8 17.7 %copy.496 = bf16[64,16,32,128]{0,3,2,1:T(8,128)(2,1)} copy(bf16[64,16,32,128]{3,2,1,0:T(8,128)(2,1)} %fusion.27) | data formatting | bytes 16777216 | tf_op jit(solution)/shard_map/convert_element_type | solution.py:248
  1320.4 15.3 %copy.497 = bf16[8,8,8,64,2,4,16]{3,6,5,4,2,1,0:T(8,128)(2,1)} copy(bf16[8,8,8,64,2,4,16]{3,6,2,5,1,4,0:T(8,128)(2,1)} %bitcast.373) | data formatting | bytes 16777216 | tf_op jit(solution)/shard_map/transpose | solution.py:126
  1335.8 26.7 %gather_fusion.4 = bf16[1024,64,128]{1,2,0:T(8,128)(2,1)} fusion(bf16[512,64,128]{1,2,0:T(8,128)(2,1)} %bitcast.371, s32[1024]{0:T(1024)S(1)} %copy-done.3), kind=kCustom, calls=%fused_computation.4 | custom fusion | bytes 33558528 | tf_op jit(solution)/shard_map/jit(_take)/gather | solution.py:250
  1362.4 30.4 %copy.499 = bf16[256,4,64,128]{3,2,1,0:T(8,128)(2,1)} copy(bf16[256,4,64,128]{2,3,1,0:T(8,128)(2,1)} %bitcast.370) | data formatting | bytes 33554432 | tf_op jit(solution)/shard_map/jit(_take)/gather | solution.py:250
  1392.8 22.2 %fusion.55 = bf16[256,64,128]{2,1,0:T(8,128)(2,1)} fusion(bf16[256,4,128,128]{3,2,1,0:T(8,128)(2,1)} %bitcast.408, bf16[256,4,64,128]{3,2,1,0:T(8,128)(2,1)} %copy.499, pred[256,4]{1,0:T(8,128)(4,1)S(1)} %bitcast.404), kind=kOutput, calls=%fused_computation.116 | convolution fusion | flops 2160066560 | bytes 54526976 | tf_op jit(solution)/shard_map/nhcx,nhpx->ncp/dot_general | solution.py:100
  1419.4 93.2 %all-to-all-done.12 = bf16[256,64,128]{2,1,0:T(8,128)(2,1)} async-done(((bf16[256,64,128]{2,1,0:T(8,128)(2,1)}), bf16[256,64,128]{2,1,0:T(8,128)(2,1)}, u32[]{:S(2)}, u32[]{:S(2)}) %all-to-all-start.12) | async-done | bytes 4194336 | tf_op jit(solution)/shard_map/all_to_all | solution.py:191
  (355 shorter events, 317.1 us)
Async XLA Ops:
  0.0 24.6 %copy-start = (bf16[128,64,128]{2,1,0:T(8,128)(2,1)S(1)}, bf16[128,64,128]{2,1,0:T(8,128)(2,1)}, u32[]{:S(2)}) copy-start(bf16[128,64,128]{2,1,0:T(8,128)(2,1)} %param.9) | copy-start | bytes 6291460
  1.7 0.8 copy-start.10
  5.5 14.4 all-to-all-start.2
  19.9 11.9 all-to-all-start
  31.9 110.6 %copy-start.4 = (s32[32,8,4]{1,2,0:T(4,128)}, s32[32,8,4]{1,2,0:T(4,128)S(1)}, u32[]{:S(2)}) copy-start(s32[32,8,4]{1,2,0:T(4,128)S(1)} %all-to-all-done) | copy-start | bytes 12292
  31.9 13.2 all-to-all-start.1
  45.0 97.5 %all-to-all-start.3 = ((bf16[256,64,128]{2,1,0:T(8,128)(2,1)}), bf16[256,64,128]{2,1,0:T(8,128)(2,1)}, u32[]{:S(2)}, u32[]{:S(2)}) async-start(bf16[256,64,128]{2,1,0:T(8,128)(2,1)} %select_select_fusion), calls=%async_computation.3 | async-start | bytes 8388608 | tf_op jit(solution)/shard_map/all_to_all | solution.py:219
  461.5 53.5 %all-to-all-start.4 = ((bf16[4,2,262144]{2,1,0:T(2,128)(2,1)}), bf16[4,2,262144]{2,1,0:T(2,128)(2,1)}, u32[]{:S(2)}, u32[]{:S(2)}) async-start(bf16[4,2,262144]{2,1,0:T(2,128)(2,1)} %reshape.1012), calls=%async_computation.4 | async-start | bytes 8388608 | tf_op jit(solution)/shard_map/all_to_all | solution.py:17
  674.4 31.2 %copy-start.6 = (f32[128,32,2]{0,1,2:T(8,128)S(1)}, f32[128,32,2]{0,1,2:T(8,128)}, u32[]{:S(2)}) copy-start(f32[128,32,2]{0,1,2:T(8,128)} %get-tuple-element.228) | copy-start | bytes 98308
  674.4 31.2 %copy-start.9 = (f32[2,64]{1,0:T(2,128)S(1)}, f32[2,64]{1,0:T(2,128)}, u32[]{:S(2)}) copy-start(f32[2,64]{1,0:T(2,128)} %param.15) | copy-start | bytes 1540
  674.4 31.8 %copy-start.8 = (bf16[2,64,64]{2,1,0:T(8,128)(2,1)S(1)}, bf16[2,64,64]{2,1,0:T(8,128)(2,1)}, u32[]{:S(2)}) copy-start(bf16[2,64,64]{2,1,0:T(8,128)(2,1)} %param.14) | copy-start | bytes 49156
  700.5 53.2 %all-to-all-start.7 = ((bf16[4,2,262144]{2,1,0:T(2,128)(2,1)}), bf16[4,2,262144]{2,1,0:T(2,128)(2,1)}, u32[]{:S(2)}, u32[]{:S(2)}) async-start(bf16[4,2,262144]{2,1,0:T(2,128)(2,1)} %reshape.1018), calls=%async_computation.7 | async-start | bytes 8388608 | tf_op jit(solution)/shard_map/all_to_all | solution.py:166
  852.3 20.5 %copy-start.2 = (bf16[64,16,32,128]{3,2,1,0:T(8,128)(2,1)}, bf16[64,16,32,128]{3,2,1,0:T(8,128)(2,1)S(1)}, u32[]{:S(2)}) copy-start(bf16[64,16,32,128]{3,2,1,0:T(8,128)(2,1)S(1)} %fusion.24) | copy-start | bytes 25165828
  1146.1 31.0 %copy-start.5 = (s32[32,8,4]{1,2,0:T(4,128)S(1)}, s32[32,8,4]{1,2,0:T(4,128)}, u32[]{:S(2)}) copy-start(s32[32,8,4]{1,2,0:T(4,128)} %copy-done.4) | copy-start | bytes 12292
  1172.1 53.2 %all-to-all-start.11 = ((bf16[4,2,262144]{2,1,0:T(2,128)(2,1)}), bf16[4,2,262144]{2,1,0:T(2,128)(2,1)}, u32[]{:S(2)}, u32[]{:S(2)}) async-start(bf16[4,2,262144]{2,1,0:T(2,128)(2,1)} %reshape.1026), calls=%async_computation.11 | async-start | bytes 8388608 | tf_op jit(solution)/shard_map/all_to_all | solution.py:166
  1234.7 22.3 %copy-start.12 = (f32[64]{0:T(128)S(1)}, f32[64]{0:T(128)}, u32[]{:S(2)}) copy-start(f32[64]{0:T(128)} %get-tuple-element.232) | copy-start | bytes 772
  1320.4 15.3 %copy-start.3 = (s32[1024]{0:T(1024)S(1)}, s32[1024]{0:T(1024)}, u32[]{:S(2)}) copy-start(s32[1024]{0:T(1024)} %broadcast_clamp_fusion) | copy-start | bytes 12292
  1362.4 30.4 %copy-start.7 = (pred[32,8,4]{2,1,0:T(8,128)(4,1)S(1)}, pred[32,8,4]{2,1,0:T(8,128)(4,1)}, u32[]{:S(2)}) copy-start(pred[32,8,4]{2,1,0:T(8,128)(4,1)} %copy.523) | copy-start | bytes 3076
  1392.8 25.8 %copy-start.11 = (s32[128]{0:T(128)S(1)}, s32[128]{0:T(128)}, u32[]{:S(2)}) copy-start(s32[128]{0:T(128)} %copy-done.10) | copy-start | bytes 1540
  1392.8 127.2 %copy-start.1 = (bf16[128,64,128]{2,1,0:T(8,128)(2,1)S(1)}, bf16[128,64,128]{2,1,0:T(8,128)(2,1)}, u32[]{:S(2)}) copy-start(bf16[128,64,128]{2,1,0:T(8,128)(2,1)} %param.9) | copy-start | bytes 6291460
  1415.1 97.5 %all-to-all-start.12 = ((bf16[256,64,128]{2,1,0:T(8,128)(2,1)}), bf16[256,64,128]{2,1,0:T(8,128)(2,1)}, u32[]{:S(2)}, u32[]{:S(2)}) async-start(bf16[256,64,128]{2,1,0:T(8,128)(2,1)} %fusion.55), calls=%async_computation.12 | async-start | bytes 8388608 | tf_op jit(solution)/shard_map/all_to_all | solution.py:191
